TPU v7x, 32 devices: a whole 2x2x4 slice. The times are simulated.
32 devices in a mesh: dp: 2 (over y), tm: 8 (over z, core), height: 2 (over x).
Axes of the slice: x: 2, y: 2, z: 4, core: 2. Of those that a mesh axis runs over, the one named last changes fastest.
Arguments:
- clip_input: bfloat16 [2, 32, 8, 96, 128], P('dp', 'tm', 'height'), may hold values from -6 to 6
- cotangent: bfloat16 [2, 32, 8, 96, 128], P('dp', 'tm', 'height'), may hold values from -6 to 6
- first_kernel: bfloat16 [2592, 96], replicated, may hold values from -0.125 to 0.125
- second_kernel: bfloat16 [2592, 96], replicated, may hold values from -0.125 to 0.125
Outputs:
- block_output: float32 [2, 32, 8, 96, 128], P('dp', 'tm', 'height')
- input_grad: float32 [2, 32, 8, 96, 128], P('dp', 'tm', 'height')
- first_grad: float32 [2592, 96], P('dp')
- second_grad: float32 [2592, 96], P('dp')
All inputs are finite; a program needn't handle non-finite values.
Results may differ from a plain program's by a relative error of at most 0.0048.
Values may be sent and summed in bfloat16 or wider, within the bound.
A program may use at most 64 MiB of HBM per device.

v0:
```python
import math
import jax
import jax.numpy as jnp
from jax import lax
from jax.sharding import PartitionSpec as P

EPSILON = 1e-06


def extended_2(array, sides, width):
    for axis, dim in sides:
        peers, length = (lax.axis_size(axis), array.shape[dim])
        up = [(i, (i + 1) % peers) for i in range(peers - 1)]
        down = [(j, i) for i, j in up]
        last = lax.slice_in_dim(array, length - width, length, axis=dim)
        first = lax.slice_in_dim(array, 0, width, axis=dim)
        before = lax.ppermute(last, axis, up)
        after = lax.ppermute(first, axis, down)
        array = jnp.concatenate([before, array, after], axis=dim)
    return array


def passed_along(array, axis, by):
    peers = lax.axis_size(axis)
    pairs = [(i, i + by) for i in range(peers) if 0 <= i + by < peers]
    return lax.ppermute(array, axis, pairs)


def norm_silu(field):
    factor = lax.rsqrt(jnp.mean(field * field, axis=2, keepdims=True) + EPSILON)
    return jax.nn.silu(field * factor)


def pad_rows(extended):
    rimmed = extended_2(extended, (("height", 1),), 1)
    return jnp.pad(rimmed, ((0, 0), (0, 0), (0, 0), (1, 1)))


def time_stack(padded, tap_row, tap_col, frames):
    row_count = padded.shape[1] - 2
    col_count = padded.shape[3] - 2
    window = padded[:, tap_row : tap_row + row_count, :, tap_col : tap_col + col_count]
    return jnp.concatenate([window[offset : offset + frames] for offset in range(3)], axis=2)


def local_conv(padded, kernel, frames):
    channels = padded.shape[2]
    summed = None
    for tap_row in range(3):
        for tap_col in range(3):
            stacked = time_stack(padded, tap_row, tap_col, frames)
            weight = kernel[:, tap_row, tap_col].reshape(3 * channels, kernel.shape[4])
            partial_sum = jnp.einsum(
                "frkw,kd->frdw", stacked, weight, preferred_element_type=jnp.float32
            )
            summed = partial_sum if summed is None else summed + partial_sum
    return summed


def kernel_grad(padded, grad_out, frames):
    channels = padded.shape[2]
    row_list = []
    for tap_row in range(3):
        col_list = []
        for tap_col in range(3):
            stacked = time_stack(padded, tap_row, tap_col, frames)
            piece = jnp.einsum(
                "frkw,frdw->kd", stacked, grad_out, preferred_element_type=jnp.float32
            )
            col_list.append(piece.reshape(3, channels, grad_out.shape[2]))
        row_list.append(jnp.stack(col_list, axis=1))
    gathered = jnp.stack(row_list, axis=1)
    return gathered.reshape(27 * channels, grad_out.shape[2])


def flipped(kernel):
    return jnp.swapaxes(kernel[::-1, ::-1, ::-1], 3, 4)


def local(clip_input, cotangent, first_kernel, second_kernel):
    frames = clip_input.shape[1]
    channels = clip_input.shape[3]
    source = clip_input[0]
    upstream = cotangent[0]
    kernel_one = first_kernel.reshape(3, 3, 3, channels, channels)
    kernel_two = second_kernel.reshape(3, 3, 3, channels, channels)

    def extend_back(block):
        earlier = passed_along(block[frames - 2 :], "tm", 1)
        return pad_rows(jnp.concatenate([earlier, block], axis=0))

    def extend_ahead(block):
        later = passed_along(block[:2], "tm", -1)
        return pad_rows(jnp.concatenate([block, later], axis=0))

    source_float = source.astype(jnp.float32)
    first_act = norm_silu(source_float).astype(jnp.bfloat16)
    first_padded = extend_back(first_act)
    middle = local_conv(first_padded, kernel_one, frames)
    second_act = norm_silu(middle).astype(jnp.bfloat16)
    second_padded = extend_back(second_act)
    branch = local_conv(second_padded, kernel_two, frames)
    block_output = source_float + branch
    second_back = local_conv(extend_ahead(upstream), flipped(kernel_two), frames)
    unused, pull_mid = jax.vjp(norm_silu, middle)
    middle_grad = pull_mid(second_back)[0].astype(jnp.bfloat16)
    first_back = local_conv(extend_ahead(middle_grad), flipped(kernel_one), frames)
    unused, pull_src = jax.vjp(norm_silu, source_float)
    input_grad = upstream.astype(jnp.float32) + pull_src(first_back)[0]
    positions = (
        frames
        * source.shape[1]
        * source.shape[3]
        * lax.axis_size("dp")
        * lax.axis_size("tm")
        * lax.axis_size("height")
    )
    factor = 1.0 / math.sqrt(positions)
    first_term = kernel_grad(first_padded, middle_grad, frames) * factor
    second_term = kernel_grad(second_padded, upstream, frames) * factor
    first_whole, second_whole = lax.psum((first_term, second_term), ("tm", "height"))
    first_grad, second_grad = (
        lax.psum_scatter(first_whole, "dp", scatter_dimension=0, tiled=True),
        lax.psum_scatter(second_whole, "dp", scatter_dimension=0, tiled=True),
    )
    return (block_output[None], input_grad[None], first_grad, second_grad)


def solution(mesh):
    return jax.shard_map(
        local,
        mesh=mesh,
        in_specs=(
            P("dp", "tm", "height", None, None),
            P("dp", "tm", "height", None, None),
            P(),
            P(),
        ),
        out_specs=(
            P("dp", "tm", "height", None, None),
            P("dp", "tm", "height", None, None),
            P("dp", None),
            P("dp", None),
        ),
        check_vma=False,
    )
```

profile of v0, /device:TPU:0, one launch (start us, length us, event | category | flops | bytes accessed | tf_op | source)
XLA Modules:
  0.0 240.6 jit_solution(6959624439068643985)
XLA Ops:
  8.2 1.3 collective-permute-start.6
  10.6 1.2 fusion.124
  11.9 3.2 %collective-permute-start = (bf16[2,4,96,128]{3,2,1,0:T(8,128)(2,1)S(1)}, bf16[2,4,96,128]{3,2,1,0:T(8,128)(2,1)S(1)}, u32[]{:S(2)}, u32[]{:S(2)}) collective-permute-start(bf16[2,4,96,128]{3,2,1,0:T(8,128)(2,1)S(1)} %slice.856), channel_id=1, source_target_pairs={{0,2},{2,4},{4,6},{6,8},{8,10},{10,12},{12,14},{1,3},{3,5},{5,7},{... | collective-permute-start | bytes 589832 | tf_op jit(solution)/shard_map/ppermute | solution.py:26
  25.4 4.9 %collective-permute-start.7 = (bf16[6,1,96,128]{3,2,1,0:T(8,128)(2,1)S(1)}, bf16[6,1,96,128]{3,2,1,0:T(8,128)(2,1)S(1)}, u32[]{:S(2)}, u32[]{:S(2)}) collective-permute-start(bf16[6,1,96,128]{3,2,1,0:T(8,128)(2,1)S(1)} %get-tuple-element.150), channel_id=1, source_target_pairs={{0,1},{2,3},{4,5},{6,7},{8,9},{10,11},{12,13},{14,15},{16,17},{18,... | collective-permute-start | bytes 442376 | tf_op jit(solution)/shard_map/ppermute | solution.py:17
  30.3 1.3 collective-permute-start.8
  31.6 1.3 collective-permute-start.2
  32.9 4.6 %collective-permute-start.1 = (bf16[6,1,96,128]{3,2,1,0:T(8,128)(2,1)S(1)}, bf16[6,1,96,128]{3,2,1,0:T(8,128)(2,1)S(1)}, u32[]{:S(2)}, u32[]{:S(2)}) collective-permute-start(bf16[6,1,96,128]{3,2,1,0:T(8,128)(2,1)S(1)} %get-tuple-element.159), channel_id=1, source_target_pairs={{0,1},{2,3},{4,5},{6,7},{8,9},{10,11},{12,13},{14,15},{16,17},{18,... | collective-permute-start | bytes 442376 | tf_op jit(solution)/shard_map/ppermute | solution.py:17
  37.6 1.3 collective-permute-done.8
  39.9 2.0 fusion.211
  43.0 2.1 fusion.213
  62.3 1.3 collective-permute-start.9
  63.6 3.0 %collective-permute-start.3 = (bf16[2,4,96,128]{3,2,1,0:T(8,128)(2,1)S(1)}, bf16[2,4,96,128]{3,2,1,0:T(8,128)(2,1)S(1)}, u32[]{:S(2)}, u32[]{:S(2)}) collective-permute-start(bf16[2,4,96,128]{3,2,1,0:T(8,128)(2,1)S(1)} %slice.896), channel_id=1, source_target_pairs={{0,2},{2,4},{4,6},{6,8},{8,10},{10,12},{12,14},{1,3},{3,5},{5,7},{... | collective-permute-start | bytes 589832 | tf_op jit(solution)/shard_map/ppermute | solution.py:26
  68.7 1.3 collective-permute-start.5
  70.0 4.6 %collective-permute-start.4 = (bf16[6,1,96,128]{3,2,1,0:T(8,128)(2,1)S(1)}, bf16[6,1,96,128]{3,2,1,0:T(8,128)(2,1)S(1)}, u32[]{:S(2)}, u32[]{:S(2)}) collective-permute-start(bf16[6,1,96,128]{3,2,1,0:T(8,128)(2,1)S(1)} %get-tuple-element.155), channel_id=1, source_target_pairs={{0,1},{2,3},{4,5},{6,7},{8,9},{10,11},{12,13},{14,15},{16,17},{18,... | collective-permute-start | bytes 442376 | tf_op jit(solution)/shard_map/ppermute | solution.py:17
  74.7 1.3 collective-permute-start.10
  76.0 1.5 collective-permute-start.11
  81.9 2.0 fusion.212
  95.5 1.3 fusion.16
  100.0 3.1 %fusion.210 = (bf16[4,4,96,128]{3,2,1,0:T(8,128)(2,1)S(1)}, bf16[4,4,96,128]{3,2,1,0:T(8,128)(2,1)S(1)}, bf16[4,4,96,128]{3,2,1,0:T(8,128)(2,1)S(1)}, bf16[4,4,9...) fusion(bf16[6,6,96,130]{3,2,1,0:T(8,128)(2,1)S(1)} %select_maxi, ...), kind=kLoop, calls=%fused_computation.330 | loop fusion | bytes 14155776 | tf_op jit(solution)/shard_map/slice | solution.py:43
  103.5 1.8 fusion.78
  113.9 17.9 %reduce-scatter.5.cloned.1.call-done = f32[1296,96]{1,0:T(8,128)} async-done(((f32[2592,96]{1,0:T(8,128)}), f32[1296,96]{1,0:T(8,128)}) %reduce-scatter.5.cloned.1.call-update) | async-done | bytes 497680 | tf_op jit(solution)/shard_map/reduce_scatter | solution.py:124
  132.9 96.8 %all-reduce.7.cloned.1.call-done = (f32[1296,96]{1,0:T(8,128)}, f32[1296,96]{1,0:T(8,128)}) async-done(((f32[1296,96]{1,0:T(8,128)}, f32[1296,96]{1,0:T(8,128)}), (f32[1296,96]{1,0:T(8,128)}, f32[1296,96]{1,0:T(8,128)})) %all-reduce.7.cloned.1.call-update) | async-done | bytes 995344 | tf_op jit(solution)/shard_map/psum | solution.py:121
  229.8 2.1 copy.104
  231.9 2.1 copy.105
  (242 shorter events, 62.3 us)
Async XLA Ops:
  7.2 7.9 %copy-start.2 = (bf16[2592,96]{0,1:T(8,128)(2,1)S(1)}, bf16[2592,96]{0,1:T(8,128)(2,1)}, u32[]{:S(2)}) copy-start(bf16[2592,96]{0,1:T(8,128)(2,1)} %param.6) | copy-start | bytes 1492996
  7.2 106.7 %reduce-scatter.3.cloned.1.call-start = ((), (), s32[]{:S(2)}) async-start(), calls=%async_computation.2 | async-start | bytes 1990656 | tf_op jit(solution)/shard_map/reduce_scatter | solution.py:123
  8.2 17.1 %collective-permute-start.6 = (bf16[2,4,96,128]{3,2,1,0:T(8,128)(2,1)S(1)}, bf16[2,4,96,128]{3,2,1,0:T(8,128)(2,1)S(1)}, u32[]{:S(2)}, u32[]{:S(2)}) collective-permute-start(bf16[2,4,96,128]{3,2,1,0:T(8,128)(2,1)S(1)} %slice_bitcast_fusion), channel_id=1, source_target_pairs={{2,0},{4,2},{6,4},{8,6},{10,8},{12,10},{14,12},{3,1},{5,3},{7,5},{... | collective-permute-start | bytes 589832 | tf_op jit(solution)/shard_map/ppermute | solution.py:26
  11.9 4.4 %copy-start.3 = (bf16[2592,96]{0,1:T(8,128)(2,1)S(1)}, bf16[2592,96]{0,1:T(8,128)(2,1)}, u32[]{:S(2)}) copy-start(bf16[2592,96]{0,1:T(8,128)(2,1)} %param.7) | copy-start | bytes 1492996
  11.9 19.7 %collective-permute-start = (bf16[2,4,96,128]{3,2,1,0:T(8,128)(2,1)S(1)}, bf16[2,4,96,128]{3,2,1,0:T(8,128)(2,1)S(1)}, u32[]{:S(2)}, u32[]{:S(2)}) collective-permute-start(bf16[2,4,96,128]{3,2,1,0:T(8,128)(2,1)S(1)} %slice.856), channel_id=1, source_target_pairs={{0,2},{2,4},{4,6},{6,8},{8,10},{10,12},{12,14},{1,3},{3,5},{5,7},{... | collective-permute-start | bytes 589832 | tf_op jit(solution)/shard_map/ppermute | solution.py:26
  17.6 7.8 %copy-start = (bf16[1,4,4,96,128]{4,3,2,1,0:T(8,128)(2,1)S(1)}, bf16[1,4,4,96,128]{4,3,2,1,0:T(8,128)(2,1)}, u32[]{:S(2)}) copy-start(bf16[1,4,4,96,128]{4,3,2,1,0:T(8,128)(2,1)} %param.5) | copy-start | bytes 1179652
  25.4 12.2 %collective-permute-start.7 = (bf16[6,1,96,128]{3,2,1,0:T(8,128)(2,1)S(1)}, bf16[6,1,96,128]{3,2,1,0:T(8,128)(2,1)S(1)}, u32[]{:S(2)}, u32[]{:S(2)}) collective-permute-start(bf16[6,1,96,128]{3,2,1,0:T(8,128)(2,1)S(1)} %get-tuple-element.150), channel_id=1, source_target_pairs={{0,1},{2,3},{4,5},{6,7},{8,9},{10,11},{12,13},{14,15},{16,17},{18,... | collective-permute-start | bytes 442376 | tf_op jit(solution)/shard_map/ppermute | solution.py:17
  30.3 8.6 %collective-permute-start.8 = (bf16[6,1,96,128]{3,2,1,0:T(8,128)(2,1)S(1)}, bf16[6,1,96,128]{3,2,1,0:T(8,128)(2,1)S(1)}, u32[]{:S(2)}, u32[]{:S(2)}) collective-permute-start(bf16[6,1,96,128]{3,2,1,0:T(8,128)(2,1)S(1)} %get-tuple-element.151), channel_id=1, source_target_pairs={{1,0},{3,2},{5,4},{7,6},{9,8},{11,10},{13,12},{15,14},{17,16},{19,... | collective-permute-start | bytes 442376 | tf_op jit(solution)/shard_map/ppermute | solution.py:18
  31.6 10.4 %collective-permute-start.2 = (bf16[6,1,96,128]{3,2,1,0:T(8,128)(2,1)S(1)}, bf16[6,1,96,128]{3,2,1,0:T(8,128)(2,1)S(1)}, u32[]{:S(2)}, u32[]{:S(2)}) collective-permute-start(bf16[6,1,96,128]{3,2,1,0:T(8,128)(2,1)S(1)} %get-tuple-element.158), channel_id=1, source_target_pairs={{1,0},{3,2},{5,4},{7,6},{9,8},{11,10},{13,12},{15,14},{17,16},{19,... | collective-permute-start | bytes 442376 | tf_op jit(solution)/shard_map/ppermute | solution.py:18
  32.9 9.1 %collective-permute-start.1 = (bf16[6,1,96,128]{3,2,1,0:T(8,128)(2,1)S(1)}, bf16[6,1,96,128]{3,2,1,0:T(8,128)(2,1)S(1)}, u32[]{:S(2)}, u32[]{:S(2)}) collective-permute-start(bf16[6,1,96,128]{3,2,1,0:T(8,128)(2,1)S(1)} %get-tuple-element.159), channel_id=1, source_target_pairs={{0,1},{2,3},{4,5},{6,7},{8,9},{10,11},{12,13},{14,15},{16,17},{18,... | collective-permute-start | bytes 442376 | tf_op jit(solution)/shard_map/ppermute | solution.py:17
  62.3 12.3 %collective-permute-start.9 = (bf16[2,4,96,128]{3,2,1,0:T(8,128)(2,1)S(1)}, bf16[2,4,96,128]{3,2,1,0:T(8,128)(2,1)S(1)}, u32[]{:S(2)}, u32[]{:S(2)}) collective-permute-start(bf16[2,4,96,128]{3,2,1,0:T(8,128)(2,1)S(1)} %slice.975), channel_id=1, source_target_pairs={{2,0},{4,2},{6,4},{8,6},{10,8},{12,10},{14,12},{3,1},{5,3},{7,5},{... | collective-permute-start | bytes 589832 | tf_op jit(solution)/shard_map/ppermute | solution.py:26
  63.6 5.1 %collective-permute-start.3 = (bf16[2,4,96,128]{3,2,1,0:T(8,128)(2,1)S(1)}, bf16[2,4,96,128]{3,2,1,0:T(8,128)(2,1)S(1)}, u32[]{:S(2)}, u32[]{:S(2)}) collective-permute-start(bf16[2,4,96,128]{3,2,1,0:T(8,128)(2,1)S(1)} %slice.896), channel_id=1, source_target_pairs={{0,2},{2,4},{4,6},{6,8},{8,10},{10,12},{12,14},{1,3},{3,5},{5,7},{... | collective-permute-start | bytes 589832 | tf_op jit(solution)/shard_map/ppermute | solution.py:26
  68.6 63.1 %reduce-scatter.5.cloned.1.call-start = ((), (), s32[]{:S(2)}) async-start(), calls=%async_computation.3 | async-start | bytes 1990656 | tf_op jit(solution)/shard_map/reduce_scatter | solution.py:124
  68.7 10.2 %collective-permute-start.5 = (bf16[6,1,96,128]{3,2,1,0:T(8,128)(2,1)S(1)}, bf16[6,1,96,128]{3,2,1,0:T(8,128)(2,1)S(1)}, u32[]{:S(2)}, u32[]{:S(2)}) collective-permute-start(bf16[6,1,96,128]{3,2,1,0:T(8,128)(2,1)S(1)} %get-tuple-element.154), channel_id=1, source_target_pairs={{1,0},{3,2},{5,4},{7,6},{9,8},{11,10},{13,12},{15,14},{17,16},{19,... | collective-permute-start | bytes 442376 | tf_op jit(solution)/shard_map/ppermute | solution.py:18
  70.0 8.9 %collective-permute-start.4 = (bf16[6,1,96,128]{3,2,1,0:T(8,128)(2,1)S(1)}, bf16[6,1,96,128]{3,2,1,0:T(8,128)(2,1)S(1)}, u32[]{:S(2)}, u32[]{:S(2)}) collective-permute-start(bf16[6,1,96,128]{3,2,1,0:T(8,128)(2,1)S(1)} %get-tuple-element.155), channel_id=1, source_target_pairs={{0,1},{2,3},{4,5},{6,7},{8,9},{10,11},{12,13},{14,15},{16,17},{18,... | collective-permute-start | bytes 442376 | tf_op jit(solution)/shard_map/ppermute | solution.py:17
  74.7 18.9 %collective-permute-start.10 = (bf16[6,1,96,128]{3,2,1,0:T(8,128)(2,1)S(1)}, bf16[6,1,96,128]{3,2,1,0:T(8,128)(2,1)S(1)}, u32[]{:S(2)}, u32[]{:S(2)}) collective-permute-start(bf16[6,1,96,128]{3,2,1,0:T(8,128)(2,1)S(1)} %get-tuple-element.146), channel_id=1, source_target_pairs={{0,1},{2,3},{4,5},{6,7},{8,9},{10,11},{12,13},{14,15},{16,17},{18,... | collective-permute-start | bytes 442376 | tf_op jit(solution)/shard_map/ppermute | solution.py:17
  76.0 17.7 %collective-permute-start.11 = (bf16[6,1,96,128]{3,2,1,0:T(8,128)(2,1)S(1)}, bf16[6,1,96,128]{3,2,1,0:T(8,128)(2,1)S(1)}, u32[]{:S(2)}, u32[]{:S(2)}) collective-permute-start(bf16[6,1,96,128]{3,2,1,0:T(8,128)(2,1)S(1)} %get-tuple-element.147), channel_id=1, source_target_pairs={{1,0},{3,2},{5,4},{7,6},{9,8},{11,10},{13,12},{15,14},{17,16},{19,... | collective-permute-start | bytes 442376 | tf_op jit(solution)/shard_map/ppermute | solution.py:18
  100.0 3.5 %copy-start.29 = (bf16[3,1,1,96,96]{4,3,0,2,1:T(8,128)(2,1)S(1)}, bf16[3,1,1,96,96]{4,3,0,2,1:T(8,128)(2,1)}, u32[]{:S(2)}) copy-start(bf16[3,1,1,96,96]{4,3,0,2,1:T(8,128)(2,1)} %copy.77) | copy-start | bytes 165892
  103.1 2.2 copy-start.27
  103.1 126.6 %all-reduce.7.cloned.1.call-start = ((), (), s32[]{:S(2)}) async-start(), calls=%async_computation.4 | async-start | bytes 2654208 | tf_op jit(solution)/shard_map/psum | solution.py:121
  103.4 1.9 copy-start.14
  103.5 1.9 copy-start.15
  103.5 1.9 copy-start.16
  107.8 1.2 copy-start.25
  (38 other events, 38.4 us)
Sparse Core Ops, SparseCore 0:
  68.8 24.7 reduce-scatter.2
  103.2 28.5 reduce-scatter.4
  135.4 94.3 all-reduce.6
where the time goes:
time: 242 us; the launch traced here: 241 us
  waiting for transfers between devices  116 us (48%)
  local copies, waits for them, and re-layouts  41.9 us (17%)
  starting transfers between devices  29.9 us (12%)
  matrix products  27.2 us (11%)
  between operations  15 us (6%)
  other arithmetic  10.3 us (4%)
    psum x1, waiting for transfers between devices, local(): lax.psum((first_term, second_term), ('tm', 'height'))  96.8 us
    dot_general x36, matrix products, local_conv(): jnp.einsum('frkw,kd->frdw', stacked, weight, preferred_element_type=jnp.f...  19 us
    reduce_scatter x1, waiting for transfers between devices, local(): lax.psum_scatter(second_whole, 'dp', scatter_dimension=0, tiled=True)  17.9 us
    unnamed x98, local copies, waits for them, and re-layouts  16.4 us
    ppermute x4, starting transfers between devices, extended_2(): before = lax.ppermute(last, axis, up)  15.3 us
    slice x10, local copies, waits for them, and re-layouts, time_stack(): window[offset:offset + frames]  12.6 us
    slice x22, local copies, waits for them, and re-layouts, local_conv(): weight = kernel[:, tap_row, tap_col].reshape(3 * channels, kernel.shape[4])  9.43 us
    ppermute x4, starting transfers between devices, passed_along(): return lax.ppermute(array, axis, pairs)  8.8 us
  transfers between devices with their start and end apart: 15, of which 4 were waited for; matrix products, arithmetic and copies ran while one was open for 19% of the time, Pallas kernels for 0%

commit v1 on v0

--- a/solution.py
+++ b/solution.py
@@ -5,6 +5,11 @@
 from jax.sharding import PartitionSpec as P
 
 EPSILON = 1e-06
+
+
+def axis_by_axis(value, one, other):
+    inner = lax.psum(value, one)
+    return lax.psum(inner, other)
 
 
 def extended_2(array, sides, width):
@@ -118,7 +123,7 @@
     factor = 1.0 / math.sqrt(positions)
     first_term = kernel_grad(first_padded, middle_grad, frames) * factor
     second_term = kernel_grad(second_padded, upstream, frames) * factor
-    first_whole, second_whole = lax.psum((first_term, second_term), ("tm", "height"))
+    first_whole, second_whole = axis_by_axis((first_term, second_term), "height", "tm")
     first_grad, second_grad = (
         lax.psum_scatter(first_whole, "dp", scatter_dimension=0, tiled=True),
         lax.psum_scatter(second_whole, "dp", scatter_dimension=0, tiled=True),

time: 242 us -> 253 us (1.045)
  waiting for transfers between devices: 116 us -> 123 us
  matrix products: 27.2 us -> 31.2 us
    psum x1 -> x2, waiting for transfers between devices: 96.8 us -> 104 us  [the longest x1 61.3 us: axis_by_axis(): return lax.psum(inner, other)]
    reduce_scatter x1, waiting for transfers between devices: 17.9 us -> 12.7 us  [local(): lax.psum_scatter(second_whole, 'dp', scatter_dimension=0, tiled=True)]
    dot_general x36, matrix products: 19 us -> 23 us  [local_conv(): jnp.einsum('frkw,kd->frdw', stacked, weight, preferred_element_type=jnp.f...]
    ppermute x4, waiting for transfers between devices: 1.46 us -> 4.33 us  [extended_2(): after = lax.ppermute(first, axis, down)]
    unnamed x98 -> x146, local copies, waits for them, and re-layouts: 16.4 us -> 16.1 us
  transfers between devices with their start and end apart: 15 -> 16, of which waited for: 4 -> 7; matrix products, arithmetic and copies ran while one was open for 19% -> 20% of each run, Pallas kernels for 0% -> 0%
where the time goes in v1:
time: 253 us; the launch traced here: 252 us
  waiting for transfers between devices  123 us (49%)
  local copies, waits for them, and re-layouts  42.2 us (17%)
  matrix products  31.2 us (12%)
  starting transfers between devices  29.9 us (12%)
  between operations  15.2 us (6%)
  other arithmetic  10.3 us (4%)
    psum x1, waiting for transfers between devices, axis_by_axis(): return lax.psum(inner, other)  61.3 us
    psum x1, waiting for transfers between devices, axis_by_axis(): inner = lax.psum(value, one)  42.6 us
    dot_general x36, matrix products, local_conv(): jnp.einsum('frkw,kd->frdw', stacked, weight, preferred_element_type=jnp.f...  23 us
    unnamed x146, local copies, waits for them, and re-layouts  16.1 us
    ppermute x4, starting transfers between devices, extended_2(): before = lax.ppermute(last, axis, up)  15.3 us
    slice x10, local copies, waits for them, and re-layouts, time_stack(): window[offset:offset + frames]  13.2 us
    reduce_scatter x1, waiting for transfers between devices, local(): lax.psum_scatter(second_whole, 'dp', scatter_dimension=0, tiled=True)  12.7 us
    ppermute x4, starting transfers between devices, passed_along(): return lax.ppermute(array, axis, pairs)  8.79 us
  transfers between devices with their start and end apart: 16, of which 7 were waited for; matrix products, arithmetic and copies ran while one was open for 20% of the time, Pallas kernels for 0%

profile of v1, /device:TPU:0, one launch (start us, length us, event | category | flops | bytes accessed | tf_op | source)
XLA Modules:
  0.0 252.1 jit_solution(16791902247732622381)
XLA Ops:
  7.2 1.7 slice_bitcast_fusion
  12.5 3.2 %collective-permute-start = (bf16[2,4,96,128]{3,2,1,0:T(8,128)(2,1)S(1)}, bf16[2,4,96,128]{3,2,1,0:T(8,128)(2,1)S(1)}, u32[]{:S(2)}, u32[]{:S(2)}) collective-permute-start(bf16[2,4,96,128]{3,2,1,0:T(8,128)(2,1)S(1)} %slice.856), channel_id=1, source_target_pairs={{0,2},{2,4},{4,6},{6,8},{8,10},{10,12},{12,14},{1,3},{3,5},{5,7},{... | collective-permute-start | bytes 589832 | tf_op jit(solution)/shard_map/ppermute | solution.py:31
  25.4 4.9 %collective-permute-start.7 = (bf16[6,1,96,128]{3,2,1,0:T(8,128)(2,1)S(1)}, bf16[6,1,96,128]{3,2,1,0:T(8,128)(2,1)S(1)}, u32[]{:S(2)}, u32[]{:S(2)}) collective-permute-start(bf16[6,1,96,128]{3,2,1,0:T(8,128)(2,1)S(1)} %get-tuple-element.152), channel_id=1, source_target_pairs={{0,1},{2,3},{4,5},{6,7},{8,9},{10,11},{12,13},{14,15},{16,17},{18,... | collective-permute-start | bytes 442376 | tf_op jit(solution)/shard_map/ppermute | solution.py:22
  32.9 4.6 %collective-permute-start.1 = (bf16[6,1,96,128]{3,2,1,0:T(8,128)(2,1)S(1)}, bf16[6,1,96,128]{3,2,1,0:T(8,128)(2,1)S(1)}, u32[]{:S(2)}, u32[]{:S(2)}) collective-permute-start(bf16[6,1,96,128]{3,2,1,0:T(8,128)(2,1)S(1)} %get-tuple-element.161), channel_id=1, source_target_pairs={{0,1},{2,3},{4,5},{6,7},{8,9},{10,11},{12,13},{14,15},{16,17},{18,... | collective-permute-start | bytes 442376 | tf_op jit(solution)/shard_map/ppermute | solution.py:22
  39.9 2.0 fusion.211
  43.0 2.1 fusion.213
  63.6 3.0 %collective-permute-start.3 = (bf16[2,4,96,128]{3,2,1,0:T(8,128)(2,1)S(1)}, bf16[2,4,96,128]{3,2,1,0:T(8,128)(2,1)S(1)}, u32[]{:S(2)}, u32[]{:S(2)}) collective-permute-start(bf16[2,4,96,128]{3,2,1,0:T(8,128)(2,1)S(1)} %slice.896), channel_id=1, source_target_pairs={{0,2},{2,4},{4,6},{6,8},{8,10},{10,12},{12,14},{1,3},{3,5},{5,7},{... | collective-permute-start | bytes 589832 | tf_op jit(solution)/shard_map/ppermute | solution.py:31
  70.0 4.6 %collective-permute-start.4 = (bf16[6,1,96,128]{3,2,1,0:T(8,128)(2,1)S(1)}, bf16[6,1,96,128]{3,2,1,0:T(8,128)(2,1)S(1)}, u32[]{:S(2)}, u32[]{:S(2)}) collective-permute-start(bf16[6,1,96,128]{3,2,1,0:T(8,128)(2,1)S(1)} %get-tuple-element.157), channel_id=1, source_target_pairs={{0,1},{2,3},{4,5},{6,7},{8,9},{10,11},{12,13},{14,15},{16,17},{18,... | collective-permute-start | bytes 442376 | tf_op jit(solution)/shard_map/ppermute | solution.py:22
  74.6 1.3 collective-permute-start.10
  75.9 1.5 collective-permute-start.11
  79.0 2.3 collective-permute-done.10
  81.3 2.9 %collective-permute-done.11 = bf16[6,1,96,128]{3,2,1,0:T(8,128)(2,1)S(1)} collective-permute-done((bf16[6,1,96,128]{3,2,1,0:T(8,128)(2,1)S(1)}, bf16[6,1,96,128]{3,2,1,0:T(8,128)(2,1)S(1)}, u32[]{:S(2)}, u32[]{:S(2)}) %collective-permute-start.11) | collective-permute-done | bytes 147488 | tf_op jit(solution)/shard_map/ppermute | solution.py:23
  89.6 1.9 fusion.212
  98.9 1.3 convolution_add_fusion.19
  101.2 3.6 %fusion.210 = (bf16[4,4,96,128]{3,2,1,0:T(8,128)(2,1)}, bf16[4,4,96,128]{3,2,1,0:T(8,128)(2,1)}, bf16[4,4,96,128]{3,2,1,0:T(8,128)(2,1)}, bf16[4,4,96,128]{3,2,1...) fusion(bf16[6,6,96,130]{3,2,1,0:T(8,128)(2,1)S(1)} %select_maxi, ...), kind=kLoop, calls=%fused_computation.330 | loop fusion | bytes 14155776 | tf_op jit(solution)/shard_map/slice | solution.py:48
  105.2 1.8 fusion.78
  111.2 1.3 convolution_add_fusion.15
  116.2 1.4 fusion.12
  117.6 12.7 %reduce-scatter.5.cloned.1.call-done = f32[1296,96]{1,0:T(8,128)} async-done(((f32[2592,96]{1,0:T(8,128)}), f32[1296,96]{1,0:T(8,128)}) %reduce-scatter.5.cloned.1.call-update) | async-done | bytes 497680 | tf_op jit(solution)/shard_map/reduce_scatter | solution.py:129
  130.4 2.6 %fusion.16 = f32[1,4,4,96,128]{4,3,2,1,0:T(8,128)} fusion(f32[4,4,128,96]{2,3,1,0:T(8,128)} %convolution_add_fusion.15, bf16[288,96,1,1]{1,0,3,2:T(8,128)(2,1)S(1)} %bitcast.410, bf16[1,4,4,96,128]{4,3,2,1,0:T(8,128)(2,1)S(1)} %copy-done.1, bf16[4,4,96,128]{3,2,1,0:T(8,128)(2,1)S(1)} %get-tuple-element.65, ...), kind=kOutput, calls=%fused_computation.48 | convolution fusion | flops 117374976 | bytes 3201024 | tf_op jit(solution)/shard_map/frkw,kd->frdw/dot_general | solution.py:58
  136.2 42.6 %all-reduce.11.cloned.1.call-done = (f32[1296,96]{1,0:T(8,128)}, f32[1296,96]{1,0:T(8,128)}) async-done(((f32[1296,96]{1,0:T(8,128)}, f32[1296,96]{1,0:T(8,128)}), (f32[1296,96]{1,0:T(8,128)}, f32[1296,96]{1,0:T(8,128)})) %all-reduce.11.cloned.1.call-update) | async-done | bytes 995344 | tf_op jit(solution)/shard_map/psum | solution.py:11
  180.0 61.3 %all-reduce.9.cloned.1.call-done = (f32[1296,96]{1,0:T(8,128)}, f32[1296,96]{1,0:T(8,128)}) async-done(((f32[1296,96]{1,0:T(8,128)}, f32[1296,96]{1,0:T(8,128)}), (f32[1296,96]{1,0:T(8,128)}, f32[1296,96]{1,0:T(8,128)})) %all-reduce.9.cloned.1.call-update) | async-done | bytes 995344 | tf_op jit(solution)/shard_map/psum | solution.py:12
  241.3 2.1 copy.104
  243.4 2.1 copy.105
  (293 shorter events, 68.0 us)
Async XLA Ops:
  7.2 8.6 %copy-start.20 = (bf16[2592,96]{0,1:T(8,128)(2,1)S(1)}, bf16[2592,96]{0,1:T(8,128)(2,1)}, u32[]{:S(2)}) copy-start(bf16[2592,96]{0,1:T(8,128)(2,1)} %param.6) | copy-start | bytes 1492996
  7.2 110.4 %reduce-scatter.3.cloned.1.call-start = ((), (), s32[]{:S(2)}) async-start(), calls=%async_computation.2 | async-start | bytes 1990656 | tf_op jit(solution)/shard_map/reduce_scatter | solution.py:128
  8.9 16.5 %collective-permute-start.6 = (bf16[2,4,96,128]{3,2,1,0:T(8,128)(2,1)}, bf16[2,4,96,128]{3,2,1,0:T(8,128)(2,1)S(1)}, u32[]{:S(2)}, u32[]{:S(2)}) collective-permute-start(bf16[2,4,96,128]{3,2,1,0:T(8,128)(2,1)} %slice_bitcast_fusion), channel_id=1, source_target_pairs={{2,0},{4,2},{6,4},{8,6},{10,8},{12,10},{14,12},{3,1},{5,3},{7,5},{... | collective-permute-start | bytes 589832 | tf_op jit(solution)/shard_map/ppermute | solution.py:31
  12.5 4.4 %copy-start.21 = (bf16[2592,96]{0,1:T(8,128)(2,1)S(1)}, bf16[2592,96]{0,1:T(8,128)(2,1)}, u32[]{:S(2)}) copy-start(bf16[2592,96]{0,1:T(8,128)(2,1)} %param.7) | copy-start | bytes 1492996
  12.5 19.0 %collective-permute-start = (bf16[2,4,96,128]{3,2,1,0:T(8,128)(2,1)S(1)}, bf16[2,4,96,128]{3,2,1,0:T(8,128)(2,1)S(1)}, u32[]{:S(2)}, u32[]{:S(2)}) collective-permute-start(bf16[2,4,96,128]{3,2,1,0:T(8,128)(2,1)S(1)} %slice.856), channel_id=1, source_target_pairs={{0,2},{2,4},{4,6},{6,8},{8,10},{10,12},{12,14},{1,3},{3,5},{5,7},{... | collective-permute-start | bytes 589832 | tf_op jit(solution)/shard_map/ppermute | solution.py:31
  18.2 7.1 %copy-start = (bf16[1,4,4,96,128]{4,3,2,1,0:T(8,128)(2,1)S(1)}, bf16[1,4,4,96,128]{4,3,2,1,0:T(8,128)(2,1)}, u32[]{:S(2)}) copy-start(bf16[1,4,4,96,128]{4,3,2,1,0:T(8,128)(2,1)} %param.5) | copy-start | bytes 1179652
  25.4 12.2 %collective-permute-start.7 = (bf16[6,1,96,128]{3,2,1,0:T(8,128)(2,1)S(1)}, bf16[6,1,96,128]{3,2,1,0:T(8,128)(2,1)S(1)}, u32[]{:S(2)}, u32[]{:S(2)}) collective-permute-start(bf16[6,1,96,128]{3,2,1,0:T(8,128)(2,1)S(1)} %get-tuple-element.152), channel_id=1, source_target_pairs={{0,1},{2,3},{4,5},{6,7},{8,9},{10,11},{12,13},{14,15},{16,17},{18,... | collective-permute-start | bytes 442376 | tf_op jit(solution)/shard_map/ppermute | solution.py:22
  30.3 8.6 %collective-permute-start.8 = (bf16[6,1,96,128]{3,2,1,0:T(8,128)(2,1)S(1)}, bf16[6,1,96,128]{3,2,1,0:T(8,128)(2,1)S(1)}, u32[]{:S(2)}, u32[]{:S(2)}) collective-permute-start(bf16[6,1,96,128]{3,2,1,0:T(8,128)(2,1)S(1)} %get-tuple-element.153), channel_id=1, source_target_pairs={{1,0},{3,2},{5,4},{7,6},{9,8},{11,10},{13,12},{15,14},{17,16},{19,... | collective-permute-start | bytes 442376 | tf_op jit(solution)/shard_map/ppermute | solution.py:23
  31.6 10.4 %collective-permute-start.2 = (bf16[6,1,96,128]{3,2,1,0:T(8,128)(2,1)S(1)}, bf16[6,1,96,128]{3,2,1,0:T(8,128)(2,1)S(1)}, u32[]{:S(2)}, u32[]{:S(2)}) collective-permute-start(bf16[6,1,96,128]{3,2,1,0:T(8,128)(2,1)S(1)} %get-tuple-element.160), channel_id=1, source_target_pairs={{1,0},{3,2},{5,4},{7,6},{9,8},{11,10},{13,12},{15,14},{17,16},{19,... | collective-permute-start | bytes 442376 | tf_op jit(solution)/shard_map/ppermute | solution.py:23
  32.9 9.1 %collective-permute-start.1 = (bf16[6,1,96,128]{3,2,1,0:T(8,128)(2,1)S(1)}, bf16[6,1,96,128]{3,2,1,0:T(8,128)(2,1)S(1)}, u32[]{:S(2)}, u32[]{:S(2)}) collective-permute-start(bf16[6,1,96,128]{3,2,1,0:T(8,128)(2,1)S(1)} %get-tuple-element.161), channel_id=1, source_target_pairs={{0,1},{2,3},{4,5},{6,7},{8,9},{10,11},{12,13},{14,15},{16,17},{18,... | collective-permute-start | bytes 442376 | tf_op jit(solution)/shard_map/ppermute | solution.py:22
  62.3 12.2 %collective-permute-start.9 = (bf16[2,4,96,128]{3,2,1,0:T(8,128)(2,1)S(1)}, bf16[2,4,96,128]{3,2,1,0:T(8,128)(2,1)S(1)}, u32[]{:S(2)}, u32[]{:S(2)}) collective-permute-start(bf16[2,4,96,128]{3,2,1,0:T(8,128)(2,1)S(1)} %slice.975), channel_id=1, source_target_pairs={{2,0},{4,2},{6,4},{8,6},{10,8},{12,10},{14,12},{3,1},{5,3},{7,5},{... | collective-permute-start | bytes 589832 | tf_op jit(solution)/shard_map/ppermute | solution.py:31
  63.6 5.0 %collective-permute-start.3 = (bf16[2,4,96,128]{3,2,1,0:T(8,128)(2,1)S(1)}, bf16[2,4,96,128]{3,2,1,0:T(8,128)(2,1)S(1)}, u32[]{:S(2)}, u32[]{:S(2)}) collective-permute-start(bf16[2,4,96,128]{3,2,1,0:T(8,128)(2,1)S(1)} %slice.896), channel_id=1, source_target_pairs={{0,2},{2,4},{4,6},{6,8},{8,10},{10,12},{12,14},{1,3},{3,5},{5,7},{... | collective-permute-start | bytes 589832 | tf_op jit(solution)/shard_map/ppermute | solution.py:31
  68.6 61.7 %reduce-scatter.5.cloned.1.call-start = ((), (), s32[]{:S(2)}) async-start(), calls=%async_computation.3 | async-start | bytes 1990656 | tf_op jit(solution)/shard_map/reduce_scatter | solution.py:129
  68.7 17.8 %collective-permute-start.5 = (bf16[6,1,96,128]{3,2,1,0:T(8,128)(2,1)S(1)}, bf16[6,1,96,128]{3,2,1,0:T(8,128)(2,1)S(1)}, u32[]{:S(2)}, u32[]{:S(2)}) collective-permute-start(bf16[6,1,96,128]{3,2,1,0:T(8,128)(2,1)S(1)} %get-tuple-element.156), channel_id=1, source_target_pairs={{1,0},{3,2},{5,4},{7,6},{9,8},{11,10},{13,12},{15,14},{17,16},{19,... | collective-permute-start | bytes 442376 | tf_op jit(solution)/shard_map/ppermute | solution.py:23
  70.0 16.5 %collective-permute-start.4 = (bf16[6,1,96,128]{3,2,1,0:T(8,128)(2,1)S(1)}, bf16[6,1,96,128]{3,2,1,0:T(8,128)(2,1)S(1)}, u32[]{:S(2)}, u32[]{:S(2)}) collective-permute-start(bf16[6,1,96,128]{3,2,1,0:T(8,128)(2,1)S(1)} %get-tuple-element.157), channel_id=1, source_target_pairs={{0,1},{2,3},{4,5},{6,7},{8,9},{10,11},{12,13},{14,15},{16,17},{18,... | collective-permute-start | bytes 442376 | tf_op jit(solution)/shard_map/ppermute | solution.py:22
  74.6 6.7 %collective-permute-start.10 = (bf16[6,1,96,128]{3,2,1,0:T(8,128)(2,1)S(1)}, bf16[6,1,96,128]{3,2,1,0:T(8,128)(2,1)S(1)}, u32[]{:S(2)}, u32[]{:S(2)}) collective-permute-start(bf16[6,1,96,128]{3,2,1,0:T(8,128)(2,1)S(1)} %get-tuple-element.148), channel_id=1, source_target_pairs={{0,1},{2,3},{4,5},{6,7},{8,9},{10,11},{12,13},{14,15},{16,17},{18,... | collective-permute-start | bytes 442376 | tf_op jit(solution)/shard_map/ppermute | solution.py:22
  75.9 8.3 %collective-permute-start.11 = (bf16[6,1,96,128]{3,2,1,0:T(8,128)(2,1)S(1)}, bf16[6,1,96,128]{3,2,1,0:T(8,128)(2,1)S(1)}, u32[]{:S(2)}, u32[]{:S(2)}) collective-permute-start(bf16[6,1,96,128]{3,2,1,0:T(8,128)(2,1)S(1)} %get-tuple-element.149), channel_id=1, source_target_pairs={{1,0},{3,2},{5,4},{7,6},{9,8},{11,10},{13,12},{15,14},{17,16},{19,... | collective-permute-start | bytes 442376 | tf_op jit(solution)/shard_map/ppermute | solution.py:23
  101.2 4.0 %copy-start.51 = (bf16[3,1,1,96,96]{4,3,0,2,1:T(8,128)(2,1)S(1)}, bf16[3,1,1,96,96]{4,3,0,2,1:T(8,128)(2,1)}, u32[]{:S(2)}) copy-start(bf16[3,1,1,96,96]{4,3,0,2,1:T(8,128)(2,1)} %copy.77) | copy-start | bytes 165892
  104.9 74.0 %all-reduce.11.cloned.1.call-start = ((), (), s32[]{:S(2)}) async-start(), calls=%async_computation.5 | async-start | bytes 2654208 | tf_op jit(solution)/shard_map/psum | solution.py:11
  116.2 14.2 %copy-start.1 = (bf16[1,4,4,96,128]{4,3,2,1,0:T(8,128)(2,1)S(1)}, bf16[1,4,4,96,128]{4,3,2,1,0:T(8,128)(2,1)}, u32[]{:S(2)}) copy-start(bf16[1,4,4,96,128]{4,3,2,1,0:T(8,128)(2,1)} %param.4) | copy-start | bytes 1179652
  116.2 14.2 %copy-start.52 = (bf16[3,1,1,96,96]{4,3,2,1,0:T(8,128)(2,1)S(1)}, bf16[3,1,1,96,96]{4,3,2,1,0:T(8,128)(2,1)}, u32[]{:S(2)}) copy-start(bf16[3,1,1,96,96]{4,3,2,1,0:T(8,128)(2,1)} %get-tuple-element.128) | copy-start | bytes 165892
  130.3 111.0 %all-reduce.9.cloned.1.call-start = ((), (), s32[]{:S(2)}) async-start(), calls=%async_computation.4 | async-start | bytes 2654208 | tf_op jit(solution)/shard_map/psum | solution.py:12
  130.4 2.7 %copy-start.25 = (bf16[4,4,96,128]{3,2,1,0:T(8,128)(2,1)S(1)}, bf16[4,4,96,128]{3,2,1,0:T(8,128)(2,1)}, u32[]{:S(2)}) copy-start(bf16[4,4,96,128]{3,2,1,0:T(8,128)(2,1)} %get-tuple-element.14) | copy-start | bytes 1179652
  130.4 2.7 %copy-start.26 = (bf16[4,4,96,128]{3,2,1,0:T(8,128)(2,1)S(1)}, bf16[4,4,96,128]{3,2,1,0:T(8,128)(2,1)}, u32[]{:S(2)}) copy-start(bf16[4,4,96,128]{3,2,1,0:T(8,128)(2,1)} %get-tuple-element.15) | copy-start | bytes 1179652
  (63 other events, 76.4 us)
Sparse Core Ops, SparseCore 0:
  68.7 24.6 reduce-scatter.2
  105.0 25.2 reduce-scatter.4
  132.6 46.1 all-reduce.10
  181.1 60.0 all-reduce.8
